TPU v7x, 32 devices: a whole 2x2x4 slice. The times are simulated.
32 devices in a mesh: dp: 8 (over z, x), tensor: 4 (over y, core).
Axes of the slice: x: 2, y: 2, z: 4, core: 2. Of those that a mesh axis runs over, the one named last changes fastest.
Arguments:
- patches: bfloat16 [24, 2048, 1024], P('dp', 'tensor'), may hold values from -6 to 6
- cotangent: bfloat16 [24, 2048, 1024], P('dp', 'tensor'), may hold values from -6 to 6
- empty_slots: int32 [8], replicated, may hold values from 0 to 2
- dataset_id: int32 [24], replicated, may hold values from 0 to 5
- dataset_weight: int32 [6], replicated, may hold values from 1 to 8
- query_key_value_weight: bfloat16 [3, 1024, 1024], P(None, None, 'tensor'), may hold values from -0.25 to 0.25
- qv_bias: float32 [2, 1024], P(None, 'tensor'), may hold values from -3 to 3
- output_projection_weight: bfloat16 [1024, 1024], P('tensor'), may hold values from -0.75 to 0.75
- out_bias: float32 [1024], replicated, may hold values from -2 to 2
- up_projection_weight: bfloat16 [1024, 4096], P(None, 'tensor'), may hold values from -0.1875 to 0.1875
- up_bias: float32 [4096], P('tensor'), may hold values from -2 to 2
- down_projection_weight: bfloat16 [4096, 1024], P('tensor'), may hold values from -0.09375 to 0.09375
- down_bias: float32 [1024], replicated, may hold values from -2 to 2
- attn_gain: float32 [1024], replicated, may hold values from 0.5 to 1.5
- attn_shift: float32 [1024], replicated, may hold values from -1.5 to 1.5
- mlp_gain: float32 [1024], replicated, may hold values from 0.5 to 1.5
- mlp_shift: float32 [1024], replicated, may hold values from -1.5 to 1.5
Outputs:
- block_out: bfloat16 [24, 2048, 1024], P('dp', 'tensor')
- grad_patches: bfloat16 [24, 2048, 1024], P('dp', 'tensor')
- grad_qkv_weight: float32 [3, 1024, 1024], P(None, None, 'tensor')
- grad_qv_bias: float32 [2, 1024], P(None, 'tensor')
- grad_out_weight: float32 [1024, 1024], P('tensor')
- grad_out_bias: float32 [1024], replicated
- grad_up_weight: float32 [1024, 4096], P(None, 'tensor')
- grad_up_bias: float32 [4096], P('tensor')
- grad_down_weight: float32 [4096, 1024], P('tensor')
- grad_down_bias: float32 [1024], replicated
- grad_attn_gain: float32 [1024], replicated
- grad_attn_shift: float32 [1024], replicated
- sensitivity_feedforward_scale: float32 [1024], replicated
- grad_mlp_shift: float32 [1024], replicated
All inputs are finite; a program needn't handle non-finite values.
Results may differ from a plain program's by a relative error of at most 0.02.
Values may be sent and summed in bfloat16 or wider, within the bound.
No kernel may reach another device: no remote copies, remote signals or barrier semaphores. Data moves between devices by JAX's collectives and lax.ppermute only.
A program may use at most 256 MiB of HBM per device.

v0:
```python
import jax
import jax.numpy as jnp
from jax import lax
from jax.sharding import PartitionSpec as P

HD = 64
epsilon = 1e-05


def norm_rows(source, norm_gain, norm_shift):
    row_mean = jnp.mean(source, axis=-1, keepdims=True)
    centred = source - row_mean
    spread = jnp.mean(centred * centred, axis=-1, keepdims=True)
    return centred * lax.rsqrt(spread + epsilon) * norm_gain + norm_shift


def gelu_exact(pre_act):
    return jax.nn.gelu(pre_act, approximate=False)


def split_heads(array, head_count):
    return array.reshape(array.shape[0], array.shape[1], head_count, HD)


def attend_item(operands):
    queries, key_rows, values = operands
    length, head_count, head_size = queries.shape
    qblock = min(512, length)
    score_scale = head_size ** (-0.5)
    blocks = queries.reshape(length // qblock, qblock, head_count, head_size)

    def one_block(query_block):
        scores = (
            jnp.einsum("qhd,khd->hqk", query_block, key_rows, preferred_element_type=jnp.float32)
            * score_scale
        )
        row_top = jnp.max(scores, axis=-1, keepdims=True)
        exp_scores = jnp.exp(scores - row_top)
        row_total = jnp.sum(exp_scores, axis=-1, keepdims=True)
        attn_weights = (exp_scores / row_total).astype(jnp.bfloat16)
        attended = jnp.einsum(
            "hqk,khd->qhd", attn_weights, values, preferred_element_type=jnp.float32
        )
        return (attended.astype(jnp.bfloat16), (row_top + jnp.log(row_total))[:, :, 0])

    attended, log_total = lax.map(one_block, blocks)
    return (attended.reshape(length, head_count, head_size), log_total)


def attend_back(operands):
    queries, key_rows, values, grad_attended, log_total = operands
    length, head_count, head_size = queries.shape
    qblock = min(512, length)
    score_scale = head_size ** (-0.5)
    query_blocks = queries.reshape(length // qblock, qblock, head_count, head_size)
    grad_blocks = grad_attended.reshape(length // qblock, qblock, head_count, head_size)

    def one_block(carried, block_in):
        query_block, grad_block, lse_block = block_in
        scores = (
            jnp.einsum("qhd,khd->hqk", query_block, key_rows, preferred_element_type=jnp.float32)
            * score_scale
        )
        attn_weights = jnp.exp(scores - lse_block[:, :, None])
        grad_weights = jnp.einsum(
            "qhd,khd->hqk", grad_block, values, preferred_element_type=jnp.float32
        )
        grad_scores = attn_weights * (
            grad_weights - jnp.sum(attn_weights * grad_weights, axis=-1, keepdims=True)
        )
        grad_low = grad_scores.astype(jnp.bfloat16)
        sensitivity_questions = (
            jnp.einsum("hqk,khd->qhd", grad_low, key_rows, preferred_element_type=jnp.float32)
            * score_scale
        )
        key_acc = (
            carried[0]
            + jnp.einsum("hqk,qhd->khd", grad_low, query_block, preferred_element_type=jnp.float32)
            * score_scale
        )
        value_acc = carried[1] + jnp.einsum(
            "hqk,qhd->khd",
            attn_weights.astype(jnp.bfloat16),
            grad_block,
            preferred_element_type=jnp.float32,
        )
        return ((key_acc, value_acc), sensitivity_questions)

    zero_acc = jnp.zeros((length, head_count, head_size), jnp.float32)
    (grad_keys, grad_values), grad_queries = lax.scan(
        one_block, (zero_acc, zero_acc), (query_blocks, grad_blocks, log_total)
    )
    return (grad_queries.reshape(length, head_count, head_size), grad_keys, grad_values)


def shards(
    patches,
    cotangent,
    empty_slots,
    dataset_id,
    dataset_weight,
    query_key_value_weight,
    qv_bias,
    output_projection_weight,
    out_bias,
    up_projection_weight,
    up_bias,
    down_projection_weight,
    down_bias,
    attn_gain,
    attn_shift,
    mlp_gain,
    mlp_shift,
):
    number_format = jnp.float32
    half_type = jnp.bfloat16
    slot_count = patches.shape[0]
    group_slots = empty_slots.shape[0]
    slot_index = jnp.arange(group_slots * slot_count, dtype=jnp.int32) % slot_count
    filled = jnp.repeat(slot_count - empty_slots, slot_count)
    valid_all = (slot_index < filled).astype(number_format)
    table_hits = (
        dataset_id[:, None] == jnp.arange(dataset_weight.shape[0], dtype=jnp.int32)[None, :]
    )
    numerator = jnp.sum(jnp.where(table_hits, dataset_weight[None, :], 0), axis=1).astype(
        number_format
    )
    total_items = jnp.sum(valid_all)
    total_weight = jnp.sum(valid_all * numerator)
    multiplier_whole = valid_all * numerator * total_items / total_weight
    own_start = lax.axis_index("dp") * slot_count
    own_scale = lax.dynamic_slice_in_dim(multiplier_whole, own_start, slot_count)
    own_valid = lax.dynamic_slice_in_dim(valid_all, own_start, slot_count)
    inputs = patches.astype(number_format)
    normed = norm_rows(inputs, attn_gain, attn_shift).astype(half_type)
    normalized_every = lax.all_gather(normed, "tensor", axis=1, tiled=True)
    local_width = query_key_value_weight.shape[2]
    head_count = local_width // HD
    projected_rows = jnp.einsum(
        "owz,gzh->gowh",
        normalized_every,
        query_key_value_weight,
        preferred_element_type=number_format,
    )
    queries = split_heads((projected_rows[0] + qv_bias[0]).astype(half_type), head_count)
    key_rows = split_heads(projected_rows[1].astype(half_type), head_count)
    values = split_heads((projected_rows[2] + qv_bias[1]).astype(half_type), head_count)
    attended, log_total = lax.map(attend_item, (queries, key_rows, values))
    attended_matrix = attended.reshape(slot_count, attended.shape[1], local_width)
    attn_part = jnp.einsum(
        "ifz,zp->ifp",
        attended_matrix,
        output_projection_weight,
        preferred_element_type=number_format,
    )
    attn_rows = lax.psum_scatter(
        attn_part.astype(jnp.bfloat16), "tensor", scatter_dimension=1, tiled=True
    ).astype(jnp.float32)
    residual = inputs + attn_rows + out_bias
    normed_mlp = norm_rows(residual, mlp_gain, mlp_shift).astype(half_type)
    cot_scaled = cotangent.astype(number_format) * own_scale[:, None, None]
    cot_low = cot_scaled.astype(half_type)
    normalized_perceptron_every = lax.all_gather(normed_mlp, "tensor", axis=1, tiled=True)
    hidden_pre = (
        jnp.einsum(
            "jzb,bu->jzu",
            normalized_perceptron_every,
            up_projection_weight,
            preferred_element_type=number_format,
        )
        + up_bias
    )
    gelu_out, gelu_back = jax.vjp(gelu_exact, hidden_pre)
    latent_activations = gelu_out.astype(half_type)
    perceptron_portion = jnp.einsum(
        "vuc,cy->vuy",
        latent_activations,
        down_projection_weight,
        preferred_element_type=number_format,
    )
    mlp_rows = lax.psum_scatter(
        perceptron_portion.astype(jnp.bfloat16), "tensor", scatter_dimension=1, tiled=True
    ).astype(jnp.float32)
    output = ((residual + mlp_rows + down_bias) * own_valid[:, None, None]).astype(half_type)
    adjoint_for_each_layer = lax.all_gather(cot_low, "tensor", axis=1, tiled=True)
    hidden_gradient = jnp.einsum(
        "eph,wh->epw",
        adjoint_for_each_layer,
        down_projection_weight,
        preferred_element_type=number_format,
    )
    preactivation_gradient = gelu_back(hidden_gradient)[0].astype(half_type)
    down_gradient = jnp.einsum(
        "wuf,wul->fl",
        latent_activations,
        adjoint_for_each_layer,
        preferred_element_type=number_format,
    )
    up_gradient = jnp.einsum(
        "eug,eut->gt",
        normalized_perceptron_every,
        preactivation_gradient,
        preferred_element_type=number_format,
    )
    grad_up_bias = jnp.sum(preactivation_gradient.astype(number_format), axis=(0, 1))
    norm_portion = jnp.einsum(
        "jmn,hn->jmh",
        preactivation_gradient,
        up_projection_weight,
        preferred_element_type=number_format,
    )
    grad_normed_mlp = lax.psum_scatter(
        norm_portion.astype(jnp.bfloat16), "tensor", scatter_dimension=1, tiled=True
    ).astype(jnp.float32)
    mlp_norm_back = jax.vjp(norm_rows, residual, mlp_gain, mlp_shift)[1]
    grad_resid_norm, sensitivity_feedforward_scale, grad_mlp_shift = mlp_norm_back(grad_normed_mlp)
    grad_residual = cot_scaled + grad_resid_norm
    grad_out_bias = jnp.sum(grad_residual, axis=(0, 1))
    grad_down_bias = jnp.sum(cot_scaled, axis=(0, 1))
    residual_gradient_every = lax.all_gather(
        grad_residual.astype(half_type), "tensor", axis=1, tiled=True
    )
    grad_attended = jnp.einsum(
        "xmn,wn->xmw",
        residual_gradient_every,
        output_projection_weight,
        preferred_element_type=number_format,
    ).astype(half_type)
    grad_out = jnp.einsum(
        "ift,ifr->tr",
        attended_matrix,
        residual_gradient_every,
        preferred_element_type=number_format,
    )
    grad_queries, grad_keys, grad_values = lax.map(
        attend_back, (queries, key_rows, values, split_heads(grad_attended, head_count), log_total)
    )
    flat_shape = (slot_count, grad_queries.shape[1], local_width)
    projection_gradient = jnp.stack(
        [
            grad_queries.reshape(flat_shape).astype(half_type),
            grad_keys.reshape(flat_shape).astype(half_type),
            grad_values.reshape(flat_shape).astype(half_type),
        ]
    )
    query_key_value_gradient = jnp.einsum(
        "ktr,jktq->jrq", normalized_every, projection_gradient, preferred_element_type=number_format
    )
    grad_qv = jnp.stack(
        [
            jnp.sum(projection_gradient[0].astype(number_format), axis=(0, 1)),
            jnp.sum(projection_gradient[2].astype(number_format), axis=(0, 1)),
        ]
    )
    normed_part = jnp.einsum(
        "vbmk,vxk->bmx",
        projection_gradient,
        query_key_value_weight,
        preferred_element_type=number_format,
    )
    grad_normed = lax.psum_scatter(
        normed_part.astype(jnp.bfloat16), "tensor", scatter_dimension=1, tiled=True
    ).astype(jnp.float32)
    attn_norm_back = jax.vjp(norm_rows, inputs, attn_gain, attn_shift)[1]
    grad_input_norm, grad_attn_gain, grad_attn_shift = attn_norm_back(grad_normed)
    grad_inputs = (grad_residual + grad_input_norm).astype(half_type)
    summed = (
        lax.psum(query_key_value_gradient.astype(jnp.bfloat16), "dp").astype(jnp.float32),
        lax.psum(grad_qv.astype(jnp.bfloat16), "dp").astype(jnp.float32),
        lax.psum(grad_out.astype(jnp.bfloat16), "dp").astype(jnp.float32),
        lax.psum(up_gradient.astype(jnp.bfloat16), "dp").astype(jnp.float32),
        lax.psum(grad_up_bias.astype(jnp.bfloat16), "dp").astype(jnp.float32),
        lax.psum(down_gradient.astype(jnp.bfloat16), "dp").astype(jnp.float32),
    )
    small_sums = lax.psum(
        (
            grad_attn_gain,
            grad_attn_shift,
            sensitivity_feedforward_scale,
            grad_mlp_shift,
            grad_out_bias,
            grad_down_bias,
        ),
        ("dp", "tensor"),
    )
    return (
        output,
        grad_inputs,
        summed[0] / total_items,
        summed[1] / total_items,
        summed[2] / total_items,
        small_sums[4] / total_items,
        summed[3] / total_items,
        summed[4] / total_items,
        summed[5] / total_items,
        small_sums[5] / total_items,
        small_sums[0] / total_items,
        small_sums[1] / total_items,
        small_sums[2] / total_items,
        small_sums[3] / total_items,
    )


def solution(mesh):
    placed = (
        P("dp", "tensor", None),
        P("dp", "tensor", None),
        P(),
        P(),
        P(),
        P(None, None, "tensor"),
        P(None, "tensor"),
        P("tensor", None),
        P(),
        P(None, "tensor"),
        P("tensor"),
        P("tensor", None),
        P(),
        P(),
        P(),
        P(),
        P(),
    )
    return jax.shard_map(
        shards,
        mesh=mesh,
        in_specs=placed,
        out_specs=(
            P("dp", "tensor", None),
            P("dp", "tensor", None),
            P(None, None, "tensor"),
            P(None, "tensor"),
            P("tensor", None),
            P(),
            P(None, "tensor"),
            P("tensor"),
            P("tensor", None),
            P(),
            P(),
            P(),
            P(),
            P(),
        ),
        check_vma=False,
    )
```

profile of v0, /device:TPU:0, one launch (start us, length us, event | category | flops | bytes accessed | tf_op | source)
XLA Modules:
  0.0 1974.1 jit_solution(18060391247935320922)
XLA Ops:
  16.7 84.7 %all-gather.5.cloned.1.call-done = bf16[3,2048,1024]{2,1,0:T(8,128)(2,1)} async-done(((bf16[3,512,1024]{2,1,0:T(8,128)(2,1)}), bf16[3,2048,1024]{2,1,0:T(8,128)(2,1)}) %all-gather.5.cloned.1.call-update) | async-done | bytes 12582928 | tf_op jit(solution)/shard_map/all_gather | solution.py:136
  101.4 17.1 fusion.58
  123.4 11.4 fusion.102
  144.1 192.9 %while.54 = (s32[]{:T(128)}, bf16[3,2048,4,64]{1,3,2,0:T(8,128)(2,1)}, f32[3,4,4,512]{3,2,1,0:T(4,128)}, bf16[3,2048,4,64]{1,3,2,0:T(8,128)(2,1)}, bf16[3,2048,4...) while((s32[]{:T(128)}, ...), condition=%wide.region_7.8_spmd, body=%wide.region_2.7_spmd.sunk | while | flops 1111619584 | bytes 74055984 | solution.py:148
  152.4 47.4 %while.57 = (s32[]{:T(128)}, bf16[4,512,4,64]{1,3,2,0:T(8,128)(2,1)}, f32[4,4,512]{2,1,0:T(4,128)S(1)}, bf16[4,512,4,64]{1,3,2,0:T(8,128)(2,1)}, bf16[2048,4,64]...) while((s32[]{:T(128)}, bf16[4,512,4,64]{1,3,2,0:T(8,128)(2,1)}, ...), condition=%wide.region_6.6_spmd, body=%wide.region_3.5_spmd.sunk | while | flops 1111619584 | bytes 57213052 | solution.py:46
  216.6 47.4 %while.57 = (s32[]{:T(128)}, bf16[4,512,4,64]{1,3,2,0:T(8,128)(2,1)}, f32[4,4,512]{2,1,0:T(4,128)S(1)}, bf16[4,512,4,64]{1,3,2,0:T(8,128)(2,1)}, bf16[2048,4,64]...) while((s32[]{:T(128)}, bf16[4,512,4,64]{1,3,2,0:T(8,128)(2,1)}, ...), condition=%wide.region_6.6_spmd, body=%wide.region_3.5_spmd.sunk | while | flops 1111619584 | bytes 57213052 | solution.py:46
  280.8 47.4 %while.57 = (s32[]{:T(128)}, bf16[4,512,4,64]{1,3,2,0:T(8,128)(2,1)}, f32[4,4,512]{2,1,0:T(4,128)S(1)}, bf16[4,512,4,64]{1,3,2,0:T(8,128)(2,1)}, bf16[2048,4,64]...) while((s32[]{:T(128)}, bf16[4,512,4,64]{1,3,2,0:T(8,128)(2,1)}, ...), condition=%wide.region_6.6_spmd, body=%wide.region_3.5_spmd.sunk | while | flops 1111619584 | bytes 57213052 | solution.py:46
  347.1 99.1 %reduce-scatter.5.cloned.1.call-done = bf16[3,512,1024]{2,1,0:T(8,128)(2,1)} async-done(((bf16[3,2048,1024]{2,1,0:T(8,128)(2,1)}), bf16[3,512,1024]{2,1,0:T(8,128)(2,1)}) %reduce-scatter.5.cloned.1.call-update) | async-done | bytes 3145744 | tf_op jit(solution)/shard_map/reduce_scatter | solution.py:156
  465.1 73.9 %all-gather.7.cloned.1.call-done = bf16[3,2048,1024]{2,1,0:T(8,128)(2,1)} async-done(((bf16[3,512,1024]{2,1,0:T(8,128)(2,1)}), bf16[3,2048,1024]{2,1,0:T(8,128)(2,1)}) %all-gather.7.cloned.1.call-update) | async-done | bytes 12582928 | tf_op jit(solution)/shard_map/all_gather | solution.py:163
  539.1 29.6 %fusion.72 = (u8[2048,1024]{1,0:T(8,128)(4,1)}, u8[2048,1024]{1,0:T(8,128)(4,1)}, f32[3,2048,1024]{2,1,0:T(8,128)}) fusion(f32[1024]{0:T(1024)S(1)} %copy-done.41, bf16[3,2048,1024]{2,1,0:T(8,128)(2,1)} %all-gather.7.cloned.1.call-done, bf16[1024,1024]{1,0:T(8,128)(2,1)S(1)} %copy-done), kind=kOutput, calls=%fused_computation.128 | convolution fusion | flops 12968787968 | bytes 44044288 | tf_op jit(solution)/shard_map/jzb,bu->jzu/dot_general | solution.py:165
  568.7 61.6 %multiply_convert_fusion.1 = (bf16[3,2048,1024]{2,1,0:T(8,128)(2,1)}, f32[3,2048,1024]{2,1,0:T(8,128)}) fusion(f32[3,2048,1024]{2,1,0:T(8,128)} %get-tuple-element.412, f32[1024]{0:T(1024)S(1)} %copy-done.41, u8[2048,1024]{1,0:T(8,128)(4,1)} %get-tuple-element.313, u8[2048,1024]{1,0:T(8,128)(4,1)} %get-tuple-element.312), kind=kLoop, calls=%fused_computation.67 | loop fusion | flops 446693376 | bytes 67112960 | tf_op jit(solution)/shard_map/convert_element_type | solution.py:174
  630.3 32.6 %fusion.103 = (bf16[1024]{0:T(1024)(128)(2,1)}, bf16[3,2048,1024]{2,1,0:T(8,128)(2,1)}) fusion(f32[3,2048,1024]{2,1,0:T(8,128)} %get-tuple-element.399, bf16[3,2048,1024]{2,1,0:T(8,128)(2,1)} %all-gather.9.cloned.1.call-done, bf16[1024,1024]{1,0:T(8,128)(2,1)} %param.36, f32[3,2048,1024]{2,1,0:T(8,128)} %get-tuple-element.412, f32[1024]{0:T(1024)S(1)} %copy-done.41), kind=kOutput, calls=%fused_computation.192 | convolution fusion | flops 12985564160 | bytes 77600768 | tf_op jit(solution)/shard_map/eph,wh->epw/dot_general | solution.py:186
  662.9 20.4 %convolution_convert_fusion = bf16[3,2048,1024]{2,1,0:T(8,128)(2,1)} fusion(bf16[3,2048,1024]{2,1,0:T(8,128)(2,1)} %get-tuple-element.414, bf16[1024,1024]{1,0:T(8,128)(2,1)S(1)} %copy-done), kind=kOutput, calls=%fused_computation.105 | convolution fusion | flops 12891193344 | bytes 27262976 | tf_op jit(solution)/shard_map/jmn,hn->jmh/dot_general | solution.py:206
  684.8 21.3 %convolution_convert_fusion.1 = bf16[3,2048,1024]{2,1,0:T(8,128)(2,1)} fusion(bf16[3,2048,1024]{2,1,0:T(8,128)(2,1)} %get-tuple-element.398, bf16[1024,1024]{1,0:T(8,128)(2,1)S(1)} %copy-done.47), kind=kOutput, calls=%fused_computation.106 | convolution fusion | flops 12891193344 | bytes 27262976 | tf_op jit(solution)/shard_map/vuc,cy->vuy/dot_general | solution.py:175
  706.3 76.2 %reduce-scatter.9.cloned.1.call-done = bf16[3,512,1024]{2,1,0:T(8,128)(2,1)} async-done(((bf16[3,2048,1024]{2,1,0:T(8,128)(2,1)}), bf16[3,512,1024]{2,1,0:T(8,128)(2,1)}) %reduce-scatter.9.cloned.1.call-update) | async-done | bytes 3145744 | tf_op jit(solution)/shard_map/reduce_scatter | solution.py:212
  795.7 88.3 %reduce-scatter.7.cloned.1.call-done = bf16[3,512,1024]{2,1,0:T(8,128)(2,1)} async-done(((bf16[3,2048,1024]{2,1,0:T(8,128)(2,1)}), bf16[3,512,1024]{2,1,0:T(8,128)(2,1)}) %reduce-scatter.7.cloned.1.call-update) | async-done | bytes 3145744 | tf_op jit(solution)/shard_map/reduce_scatter | solution.py:181
  899.3 19.5 bitcast_convert_fusion.1
  918.9 19.0 bitcast_convert_fusion.2
  937.8 43.7 %all-gather.11.cloned.1.call-done = bf16[3,2048,1024]{2,1,0:T(8,128)(2,1)} async-done(((bf16[3,512,1024]{2,1,0:T(8,128)(2,1)}), bf16[3,2048,1024]{2,1,0:T(8,128)(2,1)}) %all-gather.11.cloned.1.call-update) | async-done | bytes 12582928 | tf_op jit(solution)/shard_map/all_gather | solution.py:220
  981.5 14.3 convolution_convert_fusion.3
  995.9 553.7 %while.56 = (s32[]{:T(128)}, bf16[3,2048,4,64]{1,3,2,0:T(8,128)(2,1)}, bf16[3,2048,4,64]{1,3,2,0:T(8,128)(2,1)}, bf16[3,2048,4,64]{1,3,2,0:T(8,128)(2,1)}, bf16[...) while((s32[]{:T(128)}, ...), condition=%wide.region_22.23_spmd, body=%wide.region_18.22_spmd.sunk | while | flops 2737436672 | bytes 246014544 | solution.py:235
  1010.8 158.2 %while.58 = (s32[]{:T(128)}, f32[2048,4,64]{0,2,1:T(8,128)}, f32[2048,4,64]{0,2,1:T(8,128)}, bf16[4,512,4,64]{1,3,2,0:T(8,128)(2,1)}, bf16[4,512,4,64]{1,3,2,0:T...) while((s32[]{:T(128)}, f32[2048,4,64]{0,2,1:T(8,128)}, ...), condition=%wide.region_21.21_spmd.clone, body=%wide.region_19.20_spmd.clone.sunk | while | flops 2737436672 | bytes 206102832 | solution.py:90
  1028.9 10.6 multiply_convert_fusion.4
  1068.4 10.6 multiply_convert_fusion.4
  1195.3 158.2 %while.58 = (s32[]{:T(128)}, f32[2048,4,64]{0,2,1:T(8,128)}, f32[2048,4,64]{0,2,1:T(8,128)}, bf16[4,512,4,64]{1,3,2,0:T(8,128)(2,1)}, bf16[4,512,4,64]{1,3,2,0:T...) while((s32[]{:T(128)}, f32[2048,4,64]{0,2,1:T(8,128)}, ...), condition=%wide.region_21.21_spmd.clone, body=%wide.region_19.20_spmd.clone.sunk | while | flops 2737436672 | bytes 206102832 | solution.py:90
  1379.8 158.2 %while.58 = (s32[]{:T(128)}, f32[2048,4,64]{0,2,1:T(8,128)}, f32[2048,4,64]{0,2,1:T(8,128)}, bf16[4,512,4,64]{1,3,2,0:T(8,128)(2,1)}, bf16[4,512,4,64]{1,3,2,0:T...) while((s32[]{:T(128)}, f32[2048,4,64]{0,2,1:T(8,128)}, ...), condition=%wide.region_21.21_spmd.clone, body=%wide.region_19.20_spmd.clone.sunk | while | flops 2737436672 | bytes 206102832 | solution.py:90
  1573.3 13.9 fusion.86
  1588.6 15.4 bitcast_convert_fusion
  1609.1 22.8 %all-reduce.1 = (bf16[2,256]{1,0:T(2,128)(2,1)S(1)}, bf16[1024]{0:T(1024)(128)(2,1)S(1)}) all-reduce(bf16[2,256]{1,0:T(2,128)(2,1)S(1)} %pad_maximum_fusion.7, bf16[1024]{0:T(1024)(128)(2,1)S(1)} %copy-done.45), channel_id=1, replica_groups=mesh['dp'=8,'tensor'=4] {'dp'}, use_global_device_ids=true, to_apply=%region_29.30 | all-reduce | flops 1536 | bytes 6144 | tf_op jit(solution)/shard_map/psum | solution.py:269
  1634.4 167.8 %all-reduce.5.cloned.1.call-done = (bf16[3,1024,256]{1,2,0:T(8,128)(2,1)}, bf16[256,1024]{1,0:T(8,128)(2,1)}, bf16[1024,1024]{1,0:T(8,128)(2,1)}, bf16[1024,1024]{1,0:T(8,128)(2,1)}) async-done(((bf16[3,1024,256]{1,2,0:T(8,128)(2,1)}, bf16[256,1024]{1,0:T(8,128)(2,1)}, bf16[1024,1024]{1,0:T(8,128)(2,1)}, bf16[1024,1024]{1,0:T(8,128)(2,1)}), (bf16[3,1024,256]{1,2,0:T(8,128)(2,1)}, ...) | async-done | bytes 6291472 | tf_op jit(solution)/shard_map/psum | solution.py:268
  1821.7 81.2 %reduce-scatter.11.cloned.1.call-done = bf16[3,512,1024]{2,1,0:T(8,128)(2,1)} async-done(((bf16[3,2048,1024]{2,1,0:T(8,128)(2,1)}), bf16[3,512,1024]{2,1,0:T(8,128)(2,1)}) %reduce-scatter.11.cloned.1.call-update) | async-done | bytes 3145744 | tf_op jit(solution)/shard_map/reduce_scatter | solution.py:261
  1912.9 39.7 %all-reduce = (f32[1024]{0:T(1024)S(1)}, f32[1024]{0:T(1024)S(1)}, f32[1024]{0:T(1024)S(1)}, f32[1024]{0:T(1024)S(1)}, f32[1024]{0:T(1024)S(1)}, /*index=5*/f32[1024]{0:T(1024)S(1)}) all-reduce(f32[1024]{0:T(1024)S(1)} %copy-done.37, f32[1024]{0:T(1024)S(1)} %copy-done.38, ...), channel_id=1, replica_groups=mesh['dp'=8,'tensor'=4] {'dp','tensor'}, use_global_device_ids=true, to_apply=%region_32.33 | all-reduce | flops 6144 | bytes 49152 | tf_op jit(solution)/shard_map/psum | solution.py:275
  (534 shorter events, 883.0 us)
Async XLA Ops:
  7.2 531.9 %copy-start = (bf16[1024,1024]{1,0:T(8,128)(2,1)S(1)}, bf16[1024,1024]{1,0:T(8,128)(2,1)}, u32[]{:S(2)}) copy-start(bf16[1024,1024]{1,0:T(8,128)(2,1)} %param.34) | copy-start | bytes 6291460
  7.2 94.1 %all-gather.5.cloned.1.call-start = ((), (), s32[]{:S(2)}) async-start(), calls=%async_computation.4 | async-start | bytes 15728640 | tf_op jit(solution)/shard_map/all_gather | solution.py:136
  16.4 429.9 %reduce-scatter.5.cloned.1.call-start = ((), (), s32[]{:S(2)}) async-start(), calls=%async_computation.5 | async-start | bytes 15728640 | tf_op jit(solution)/shard_map/reduce_scatter | solution.py:156
  347.0 99.2 %copy-start.23 = (f32[1024]{0:T(1024)S(1)}, f32[1024]{0:T(1024)}, u32[]{:S(2)}) copy-start(f32[1024]{0:T(1024)} %param.33) | copy-start | bytes 12292
  347.1 106.7 %copy-start.32 = (f32[1024]{0:T(1024)S(1)}, f32[1024]{0:T(1024)}, u32[]{:S(2)}) copy-start(f32[1024]{0:T(1024)} %param.40) | copy-start | bytes 12292
  347.1 106.7 %copy-start.39 = (f32[1024]{0:T(1024)S(1)}, f32[1024]{0:T(1024)}, u32[]{:S(2)}) copy-start(f32[1024]{0:T(1024)} %param.41) | copy-start | bytes 12292
  347.1 192.0 %all-gather.7.cloned.1.call-start = ((), (), s32[]{:S(2)}) async-start(), calls=%async_computation.6 | async-start | bytes 15728640 | tf_op jit(solution)/shard_map/all_gather | solution.py:163
  456.8 82.3 %copy-start.41 = (f32[1024]{0:T(1024)S(1)}, f32[1024]{0:T(1024)}, u32[]{:S(2)}) copy-start(f32[1024]{0:T(1024)} %param.35) | copy-start | bytes 12292
  456.8 173.5 %all-gather.9.cloned.1.call-start = ((), (), s32[]{:S(2)}) async-start(), calls=%async_computation.8 | async-start | bytes 15728640 | tf_op jit(solution)/shard_map/all_gather | solution.py:185
  460.3 108.4 %copy-start.43 = (f32[3]{0:T(128)}, f32[3]{0:T(128)S(1)}, u32[]{:S(2)}) copy-start(f32[3]{0:T(128)S(1)} %dynamic_slice.47) | copy-start | bytes 40
  465.1 317.4 %reduce-scatter.9.cloned.1.call-start = ((), (), s32[]{:S(2)}) async-start(), calls=%async_computation.9 | async-start | bytes 15728640 | tf_op jit(solution)/shard_map/reduce_scatter | solution.py:212
  683.3 200.7 %reduce-scatter.7.cloned.1.call-start = ((), (), s32[]{:S(2)}) async-start(), calls=%async_computation.7 | async-start | bytes 15728640 | tf_op jit(solution)/shard_map/reduce_scatter | solution.py:181
  706.1 82.2 %copy-start.31 = (f32[3,512]{1,0:T(4,128)S(1)}, f32[3,512]{1,0:T(4,128)}, u32[]{:S(2)}) copy-start(f32[3,512]{1,0:T(4,128)} %copy-done.30) | copy-start | bytes 18436
  706.1 82.2 %copy-start.27 = (f32[3,512]{1,0:T(4,128)S(1)}, f32[3,512]{1,0:T(4,128)}, u32[]{:S(2)}) copy-start(f32[3,512]{1,0:T(4,128)} %copy-done.26) | copy-start | bytes 18436
  706.2 275.4 %all-gather.11.cloned.1.call-start = ((), (), s32[]{:S(2)}) async-start(), calls=%async_computation.10 | async-start | bytes 15728640 | tf_op jit(solution)/shard_map/all_gather | solution.py:220
  788.4 95.6 %copy-start.42 = (f32[1024]{0:T(1024)S(1)}, f32[1024]{0:T(1024)}, u32[]{:S(2)}) copy-start(f32[1024]{0:T(1024)} %param.37) | copy-start | bytes 12292
  788.4 95.6 %copy-start.44 = (f32[3]{0:T(128)S(1)}, f32[3]{0:T(128)}, u32[]{:S(2)}) copy-start(f32[3]{0:T(128)} %copy-done.43) | copy-start | bytes 40
  899.2 902.9 %all-reduce.5.cloned.1.call-start = ((), (), s32[]{:S(2)}) async-start(), calls=%async_computation.12 | async-start | bytes 12582912 | tf_op jit(solution)/shard_map/psum | solution.py:268
  918.9 62.7 %copy-start.19 = (bf16[256,1024]{1,0:T(8,128)(2,1)S(1)}, bf16[256,1024]{1,0:T(8,128)(2,1)}, u32[]{:S(2)}) copy-start(bf16[256,1024]{1,0:T(8,128)(2,1)} %param.32) | copy-start | bytes 1572868
  1028.9 17.5 copy-start.6
  1068.4 17.5 copy-start.6
  1108.0 17.5 copy-start.6
  1147.5 17.5 copy-start.6
  1587.3 315.7 %reduce-scatter.11.cloned.1.call-start = ((), (), s32[]{:S(2)}) async-start(), calls=%async_computation.11 | async-start | bytes 15728640 | tf_op jit(solution)/shard_map/reduce_scatter | solution.py:261
  1812.1 90.8 %copy-start.22 = (f32[3,512]{1,0:T(4,128)S(1)}, f32[3,512]{1,0:T(4,128)}, u32[]{:S(2)}) copy-start(f32[3,512]{1,0:T(4,128)} %copy-done.21) | copy-start | bytes 18436
  1812.1 90.8 %copy-start.34 = (f32[1024]{0:T(1024)S(1)}, f32[1024]{0:T(1024)}, u32[]{:S(2)}) copy-start(f32[1024]{0:T(1024)} %param.38) | copy-start | bytes 12292
  1818.0 89.3 %copy-start.29 = (f32[3,512]{1,0:T(4,128)S(1)}, f32[3,512]{1,0:T(4,128)}, u32[]{:S(2)}) copy-start(f32[3,512]{1,0:T(4,128)} %copy-done.28) | copy-start | bytes 18436
  1818.0 89.4 %copy-start.25 = (f32[3,512]{1,0:T(4,128)S(1)}, f32[3,512]{1,0:T(4,128)}, u32[]{:S(2)}) copy-start(f32[3,512]{1,0:T(4,128)} %copy-done.24) | copy-start | bytes 18436
  1821.7 91.2 %copy-start.35 = (f32[1024]{0:T(1024)S(1)}, f32[1024]{0:T(1024)}, u32[]{:S(2)}) copy-start(f32[1024]{0:T(1024)} %get-tuple-element.318) | copy-start | bytes 12292
  1821.7 91.2 %copy-start.36 = (f32[1024]{0:T(1024)S(1)}, f32[1024]{0:T(1024)}, u32[]{:S(2)}) copy-start(f32[1024]{0:T(1024)} %get-tuple-element.314) | copy-start | bytes 12292
  1821.7 91.2 %copy-start.37 = (f32[1024]{0:T(1024)S(1)}, f32[1024]{0:T(1024)}, u32[]{:S(2)}) copy-start(f32[1024]{0:T(1024)} %get-tuple-element.396) | copy-start | bytes 12292
  1821.7 91.2 %copy-start.38 = (f32[1024]{0:T(1024)S(1)}, f32[1024]{0:T(1024)}, u32[]{:S(2)}) copy-start(f32[1024]{0:T(1024)} %get-tuple-element.411) | copy-start | bytes 12292
  (97 other events, 587.0 us)
Sparse Core Ops, SparseCore 0:
  16.5 84.7 all-gather.4
  347.2 99.0 reduce-scatter.4
  456.9 82.0 all-gather.6
  540.5 82.0 all-gather.8
  683.4 99.0 reduce-scatter.8
  785.0 99.0 reduce-scatter.6
  899.4 82.1 all-gather.10
  1587.4 214.7 all-reduce.4
  1804.9 97.9 reduce-scatter.10
where the time goes:
time: 1990 us; the launch traced here: 1970 us
  waiting for transfers between devices  715 us (36%)
  matrix products  649 us (33%)
  other arithmetic  334 us (17%)
  local copies, waits for them, and re-layouts  196 us (10%)
  blocking collectives  62.6 us (3%)
    psum x1, waiting for transfers between devices, shards(): lax.psum(query_key_value_gradient.astype(jnp.bfloat16), 'dp')  168 us
    convert_element_type x12, other arithmetic, one_block(): grad_low = grad_scores.astype(jnp.bfloat16)  127 us
    dot_general x12, matrix products, one_block(): jnp.einsum('qhd,khd->hqk', grad_block, values, preferred_element_type=jnp...  113 us
    reduce_scatter x1, waiting for transfers between devices, shards(): lax.psum_scatter(attn_part.astype(jnp.bfloat16), 'tensor', scatter_dimens...  99.1 us
    reduce_scatter x1, waiting for transfers between devices, shards(): lax.psum_scatter(perceptron_portion.astype(jnp.bfloat16), 'tensor', scatt...  88.3 us
    all_gather x1, waiting for transfers between devices, shards(): normalized_every = lax.all_gather(normed, 'tensor', axis=1, tiled=True)  84.7 us
    dot_general x12, matrix products, one_block(): jnp.einsum('hqk,khd->qhd', grad_low, key_rows, preferred_element_type=jnp...  82.8 us
    dot_general x24, matrix products, one_block(): jnp.einsum('qhd,khd->hqk', query_block, key_rows, preferred_element_type=...  82.5 us
  transfers between devices with their start and end apart: 9, of which 8 were waited for; matrix products, arithmetic and copies ran while one was open for 11% of the time, Pallas kernels for 0%

commit v1 on v0

--- a/solution.py
+++ b/solution.py
@@ -5,6 +5,27 @@
 
 HD = 64
 epsilon = 1e-05
+
+
+def joined_along(blocks, dim):
+    shape = list(blocks.shape[1:])
+    shape[dim] *= blocks.shape[0]
+    return jnp.moveaxis(blocks, 0, dim).reshape(shape)
+
+
+def doubled(x, axis):
+    size, mine = (lax.axis_size(axis), lax.axis_index(axis))
+    pieces, bit = (x[None], 1)
+    while bit < size:
+        other = lax.ppermute(pieces, axis, [(i, i ^ bit) for i in range(size)])
+        low = mine & bit == 0
+        pieces = jnp.concatenate([jnp.where(low, pieces, other), jnp.where(low, other, pieces)])
+        bit *= 2
+    return pieces
+
+
+def doubled_up(x, axis, dim):
+    return joined_along(doubled(x, axis), dim)
 
 
 def norm_rows(source, norm_gain, norm_shift):
@@ -160,7 +181,7 @@
     normed_mlp = norm_rows(residual, mlp_gain, mlp_shift).astype(half_type)
     cot_scaled = cotangent.astype(number_format) * own_scale[:, None, None]
     cot_low = cot_scaled.astype(half_type)
-    normalized_perceptron_every = lax.all_gather(normed_mlp, "tensor", axis=1, tiled=True)
+    normalized_perceptron_every = doubled_up(normed_mlp, "tensor", 1)
     hidden_pre = (
         jnp.einsum(
             "jzb,bu->jzu",

time: 1990 us -> 2140 us (1.075)
  waiting for transfers between devices: 715 us -> 843 us
    ppermute x0 -> x2, waiting for transfers between devices: none -> 203 us  [doubled(): other = lax.ppermute(pieces, axis, [(i, i ^ bit) for i in range(size)])]
    all_gather x1 -> x0, waiting for transfers between devices: 73.9 us -> none  [shards(): lax.all_gather(normed_mlp, 'tensor', axis=1, tiled=True)]
  transfers between devices with their start and end apart: 9 -> 10, of which waited for: 8 -> 9; matrix products, arithmetic and copies ran while one was open for 11% -> 11% of each run, Pallas kernels for 0% -> 0%
where the time goes in v1:
time: 2140 us; the launch traced here: 2130 us
  waiting for transfers between devices  843 us (39%)
  matrix products  646 us (30%)
  other arithmetic  348 us (16%)
  local copies, waits for them, and re-layouts  204 us (10%)
  blocking collectives  62.6 us (3%)
    ppermute x2, waiting for transfers between devices, doubled(): other = lax.ppermute(pieces, axis, [(i, i ^ bit) for i in range(size)])  203 us
    psum x1, waiting for transfers between devices, shards(): lax.psum(query_key_value_gradient.astype(jnp.bfloat16), 'dp')  168 us
    convert_element_type x12, other arithmetic, one_block(): grad_low = grad_scores.astype(jnp.bfloat16)  127 us
    dot_general x12, matrix products, one_block(): jnp.einsum('qhd,khd->hqk', grad_block, values, preferred_element_type=jnp...  110 us
    reduce_scatter x1, waiting for transfers between devices, shards(): lax.psum_scatter(attn_part.astype(jnp.bfloat16), 'tensor', scatter_dimens...  99.2 us
    reduce_scatter x1, waiting for transfers between devices, shards(): lax.psum_scatter(perceptron_portion.astype(jnp.bfloat16), 'tensor', scatt...  88.3 us
    all_gather x1, waiting for transfers between devices, shards(): normalized_every = lax.all_gather(normed, 'tensor', axis=1, tiled=True)  84.7 us
    dot_general x12, matrix products, one_block(): jnp.einsum('hqk,khd->qhd', grad_low, key_rows, preferred_element_type=jnp...  82.8 us
  transfers between devices with their start and end apart: 10, of which 9 were waited for; matrix products, arithmetic and copies ran while one was open for 11% of the time, Pallas kernels for 0%

profile of v1, /device:TPU:0, one launch (start us, length us, event | category | flops | bytes accessed | tf_op | source)
XLA Modules:
  0.0 2130.4 jit_solution(7073875466351213030)
XLA Ops:
  16.7 84.7 %all-gather.4.cloned.1.call-done = bf16[3,2048,1024]{2,1,0:T(8,128)(2,1)} async-done(((bf16[3,512,1024]{2,1,0:T(8,128)(2,1)}), bf16[3,2048,1024]{2,1,0:T(8,128)(2,1)}) %all-gather.4.cloned.1.call-update) | async-done | bytes 12582928 | tf_op jit(solution)/shard_map/all_gather | solution.py:157
  101.4 17.1 fusion.58
  123.4 11.4 fusion.103
  144.1 202.5 %while.54 = (s32[]{:T(128)}, bf16[3,2048,4,64]{1,3,2,0:T(8,128)(2,1)}, f32[3,4,4,512]{3,2,1,0:T(4,128)}, bf16[3,2048,4,64]{1,3,2,0:T(8,128)(2,1)}, bf16[3,2048,4...) while((s32[]{:T(128)}, ...), condition=%wide.region_7.8_spmd, body=%wide.region_2.7_spmd.sunk | while | flops 1111619584 | bytes 74055984 | solution.py:169
  162.2 47.4 %while.57 = (s32[]{:T(128)}, bf16[4,512,4,64]{1,3,2,0:T(8,128)(2,1)}, f32[4,4,512]{2,1,0:T(4,128)S(1)}, bf16[4,512,4,64]{1,3,2,0:T(8,128)(2,1)}, bf16[2048,4,64]...) while((s32[]{:T(128)}, bf16[4,512,4,64]{1,3,2,0:T(8,128)(2,1)}, ...), condition=%wide.region_6.6_spmd, body=%wide.region_3.5_spmd.sunk | while | flops 1111619584 | bytes 57213052 | solution.py:67
  226.4 47.4 %while.57 = (s32[]{:T(128)}, bf16[4,512,4,64]{1,3,2,0:T(8,128)(2,1)}, f32[4,4,512]{2,1,0:T(4,128)S(1)}, bf16[4,512,4,64]{1,3,2,0:T(8,128)(2,1)}, bf16[2048,4,64]...) while((s32[]{:T(128)}, bf16[4,512,4,64]{1,3,2,0:T(8,128)(2,1)}, ...), condition=%wide.region_6.6_spmd, body=%wide.region_3.5_spmd.sunk | while | flops 1111619584 | bytes 57213052 | solution.py:67
  290.6 47.4 %while.57 = (s32[]{:T(128)}, bf16[4,512,4,64]{1,3,2,0:T(8,128)(2,1)}, f32[4,4,512]{2,1,0:T(4,128)S(1)}, bf16[4,512,4,64]{1,3,2,0:T(8,128)(2,1)}, bf16[2048,4,64]...) while((s32[]{:T(128)}, bf16[4,512,4,64]{1,3,2,0:T(8,128)(2,1)}, ...), condition=%wide.region_6.6_spmd, body=%wide.region_3.5_spmd.sunk | while | flops 1111619584 | bytes 57213052 | solution.py:67
  356.9 99.2 %reduce-scatter.5.cloned.1.call-done = bf16[3,512,1024]{2,1,0:T(8,128)(2,1)} async-done(((bf16[3,2048,1024]{2,1,0:T(8,128)(2,1)}), bf16[3,512,1024]{2,1,0:T(8,128)(2,1)}) %reduce-scatter.5.cloned.1.call-update) | async-done | bytes 3145744 | tf_op jit(solution)/shard_map/reduce_scatter | solution.py:177
  488.5 196.6 %collective-permute-done.1 = bf16[2,3,512,1024]{3,2,1,0:T(8,128)(2,1)} collective-permute-done((bf16[2,3,512,1024]{3,2,1,0:T(8,128)(2,1)}, bf16[2,3,512,1024]{3,2,1,0:T(8,128)(2,1)}, u32[]{:S(2)}, u32[]{:S(2)}) %collective-permute-start.1) | collective-permute-done | bytes 6291488 | tf_op jit(solution)/shard_map/ppermute | solution.py:20
  697.0 29.6 %fusion.72 = (u8[2048,1024]{1,0:T(8,128)(4,1)}, u8[2048,1024]{1,0:T(8,128)(4,1)}, f32[3,2048,1024]{2,1,0:T(8,128)}) fusion(f32[1024]{0:T(1024)S(1)} %copy-done.49, bf16[3,2048,1024]{2,1,0:T(8,128)(2,1)} %bitcast.217, bf16[1024,1024]{1,0:T(8,128)(2,1)S(1)} %copy-done), kind=kOutput, calls=%fused_computation.132 | convolution fusion | flops 12968787968 | bytes 44044288 | tf_op jit(solution)/shard_map/jzb,bu->jzu/dot_general | solution.py:186
  726.5 61.6 %multiply_convert_fusion.1 = (bf16[3,2048,1024]{2,1,0:T(8,128)(2,1)}, f32[3,2048,1024]{2,1,0:T(8,128)}) fusion(f32[3,2048,1024]{2,1,0:T(8,128)} %get-tuple-element.416, f32[1024]{0:T(1024)S(1)} %copy-done.49, u8[2048,1024]{1,0:T(8,128)(4,1)} %get-tuple-element.313, u8[2048,1024]{1,0:T(8,128)(4,1)} %get-tuple-element.312), kind=kLoop, calls=%fused_computation.67 | loop fusion | flops 446693376 | bytes 67112960 | tf_op jit(solution)/shard_map/convert_element_type | solution.py:195
  788.1 32.8 %fusion.104 = (bf16[1024]{0:T(1024)(128)(2,1)}, bf16[3,2048,1024]{2,1,0:T(8,128)(2,1)}) fusion(f32[3,2048,1024]{2,1,0:T(8,128)} %get-tuple-element.399, bf16[3,2048,1024]{2,1,0:T(8,128)(2,1)} %all-gather.6.cloned.1.call-done, bf16[1024,1024]{1,0:T(8,128)(2,1)} %param.36, f32[3,2048,1024]{2,1,0:T(8,128)} %get-tuple-element.416, f32[1024]{0:T(1024)S(1)} %copy-done.49), kind=kOutput, calls=%fused_computation.199 | convolution fusion | flops 12985564160 | bytes 77600768 | tf_op jit(solution)/shard_map/eph,wh->epw/dot_general | solution.py:207
  821.0 20.3 convolution_convert_fusion
  842.8 21.2 convolution_convert_fusion.1
  864.8 75.7 %reduce-scatter.9.cloned.1.call-done = bf16[3,512,1024]{2,1,0:T(8,128)(2,1)} async-done(((bf16[3,2048,1024]{2,1,0:T(8,128)(2,1)}), bf16[3,512,1024]{2,1,0:T(8,128)(2,1)}) %reduce-scatter.9.cloned.1.call-update) | async-done | bytes 3145744 | tf_op jit(solution)/shard_map/reduce_scatter | solution.py:233
  953.7 88.3 %reduce-scatter.7.cloned.1.call-done = bf16[3,512,1024]{2,1,0:T(8,128)(2,1)} async-done(((bf16[3,2048,1024]{2,1,0:T(8,128)(2,1)}), bf16[3,512,1024]{2,1,0:T(8,128)(2,1)}) %reduce-scatter.7.cloned.1.call-update) | async-done | bytes 3145744 | tf_op jit(solution)/shard_map/reduce_scatter | solution.py:202
  1057.4 19.3 bitcast_convert_fusion.2
  1076.7 18.9 bitcast_convert_fusion.1
  1095.6 44.0 %all-gather.8.cloned.1.call-done = bf16[3,2048,1024]{2,1,0:T(8,128)(2,1)} async-done(((bf16[3,512,1024]{2,1,0:T(8,128)(2,1)}), bf16[3,2048,1024]{2,1,0:T(8,128)(2,1)}) %all-gather.8.cloned.1.call-update) | async-done | bytes 12582928 | tf_op jit(solution)/shard_map/all_gather | solution.py:241
  1139.6 14.3 convolution_convert_fusion.3
  1153.8 552.1 %while.56 = (s32[]{:T(128)}, bf16[3,2048,4,64]{1,3,2,0:T(8,128)(2,1)}, bf16[3,2048,4,64]{1,3,2,0:T(8,128)(2,1)}, bf16[3,2048,4,64]{1,3,2,0:T(8,128)(2,1)}, bf16[...) while((s32[]{:T(128)}, ...), condition=%wide.region_22.23_spmd, body=%wide.region_18.22_spmd.sunk | while | flops 2737436672 | bytes 246014544 | solution.py:256
  1169.0 157.6 %while.58 = (s32[]{:T(128)}, f32[2048,4,64]{0,2,1:T(8,128)}, f32[2048,4,64]{0,2,1:T(8,128)}, bf16[4,512,4,64]{1,3,2,0:T(8,128)(2,1)}, bf16[4,512,4,64]{1,3,2,0:T...) while((s32[]{:T(128)}, f32[2048,4,64]{0,2,1:T(8,128)}, ...), condition=%wide.region_21.21_spmd.clone, body=%wide.region_19.20_spmd.clone.sunk | while | flops 2737436672 | bytes 206102832 | solution.py:111
  1186.9 10.6 multiply_convert_fusion.4
  1265.7 10.6 multiply_convert_fusion.4
  1352.9 157.6 %while.58 = (s32[]{:T(128)}, f32[2048,4,64]{0,2,1:T(8,128)}, f32[2048,4,64]{0,2,1:T(8,128)}, bf16[4,512,4,64]{1,3,2,0:T(8,128)(2,1)}, bf16[4,512,4,64]{1,3,2,0:T...) while((s32[]{:T(128)}, f32[2048,4,64]{0,2,1:T(8,128)}, ...), condition=%wide.region_21.21_spmd.clone, body=%wide.region_19.20_spmd.clone.sunk | while | flops 2737436672 | bytes 206102832 | solution.py:111
  1536.8 157.6 %while.58 = (s32[]{:T(128)}, f32[2048,4,64]{0,2,1:T(8,128)}, f32[2048,4,64]{0,2,1:T(8,128)}, bf16[4,512,4,64]{1,3,2,0:T(8,128)(2,1)}, bf16[4,512,4,64]{1,3,2,0:T...) while((s32[]{:T(128)}, f32[2048,4,64]{0,2,1:T(8,128)}, ...), condition=%wide.region_21.21_spmd.clone, body=%wide.region_19.20_spmd.clone.sunk | while | flops 2737436672 | bytes 206102832 | solution.py:111
  1729.8 13.9 fusion.87
  1745.1 15.4 bitcast_convert_fusion
  1765.5 22.8 %all-reduce.1 = (bf16[2,256]{1,0:T(2,128)(2,1)S(1)}, bf16[1024]{0:T(1024)(128)(2,1)S(1)}) all-reduce(bf16[2,256]{1,0:T(2,128)(2,1)S(1)} %pad_maximum_fusion.8, bf16[1024]{0:T(1024)(128)(2,1)S(1)} %copy-done.53), channel_id=1, replica_groups=mesh['dp'=8,'tensor'=4] {'dp'}, use_global_device_ids=true, to_apply=%region_29.30 | all-reduce | flops 1536 | bytes 6144 | tf_op jit(solution)/shard_map/psum | solution.py:290
  1790.8 167.6 %all-reduce.5.cloned.1.call-done = (bf16[3,1024,256]{1,2,0:T(8,128)(2,1)}, bf16[256,1024]{1,0:T(8,128)(2,1)}, bf16[1024,1024]{1,0:T(8,128)(2,1)}, bf16[1024,1024]{1,0:T(8,128)(2,1)}) async-done(((bf16[3,1024,256]{1,2,0:T(8,128)(2,1)}, bf16[256,1024]{1,0:T(8,128)(2,1)}, bf16[1024,1024]{1,0:T(8,128)(2,1)}, bf16[1024,1024]{1,0:T(8,128)(2,1)}), (bf16[3,1024,256]{1,2,0:T(8,128)(2,1)}, ...) | async-done | bytes 6291472 | tf_op jit(solution)/shard_map/psum | solution.py:289
  1977.9 81.3 %reduce-scatter.11.cloned.1.call-done = bf16[3,512,1024]{2,1,0:T(8,128)(2,1)} async-done(((bf16[3,2048,1024]{2,1,0:T(8,128)(2,1)}), bf16[3,512,1024]{2,1,0:T(8,128)(2,1)}) %reduce-scatter.11.cloned.1.call-update) | async-done | bytes 3145744 | tf_op jit(solution)/shard_map/reduce_scatter | solution.py:282
  2069.2 39.8 %all-reduce = (f32[1024]{0:T(1024)S(1)}, f32[1024]{0:T(1024)S(1)}, f32[1024]{0:T(1024)S(1)}, f32[1024]{0:T(1024)S(1)}, f32[1024]{0:T(1024)S(1)}, /*index=5*/f32[1024]{0:T(1024)S(1)}) all-reduce(f32[1024]{0:T(1024)S(1)} %copy-done.43, f32[1024]{0:T(1024)S(1)} %copy-done.44, ...), channel_id=1, replica_groups=mesh['dp'=8,'tensor'=4] {'dp','tensor'}, use_global_device_ids=true, to_apply=%region_32.33 | all-reduce | flops 6144 | bytes 49152 | tf_op jit(solution)/shard_map/psum | solution.py:296
  (556 shorter events, 907.1 us)
Async XLA Ops:
  7.2 689.8 %copy-start = (bf16[1024,1024]{1,0:T(8,128)(2,1)S(1)}, bf16[1024,1024]{1,0:T(8,128)(2,1)}, u32[]{:S(2)}) copy-start(bf16[1024,1024]{1,0:T(8,128)(2,1)} %param.34) | copy-start | bytes 6291460
  7.2 94.1 %all-gather.4.cloned.1.call-start = ((), (), s32[]{:S(2)}) async-start(), calls=%async_computation.4 | async-start | bytes 15728640 | tf_op jit(solution)/shard_map/all_gather | solution.py:157
  16.4 439.6 %reduce-scatter.5.cloned.1.call-start = ((), (), s32[]{:S(2)}) async-start(), calls=%async_computation.5 | async-start | bytes 15728640 | tf_op jit(solution)/shard_map/reduce_scatter | solution.py:177
  356.8 99.3 %copy-start.27 = (f32[1024]{0:T(1024)S(1)}, f32[1024]{0:T(1024)}, u32[]{:S(2)}) copy-start(f32[1024]{0:T(1024)} %param.33) | copy-start | bytes 12292
  356.8 106.2 %copy-start.37 = (f32[1024]{0:T(1024)S(1)}, f32[1024]{0:T(1024)}, u32[]{:S(2)}) copy-start(f32[1024]{0:T(1024)} %param.40) | copy-start | bytes 12292
  356.8 106.2 %copy-start.47 = (f32[1024]{0:T(1024)S(1)}, f32[1024]{0:T(1024)}, u32[]{:S(2)}) copy-start(f32[1024]{0:T(1024)} %param.41) | copy-start | bytes 12292
  356.8 431.3 %all-gather.6.cloned.1.call-start = ((), (), s32[]{:S(2)}) async-start(), calls=%async_computation.7 | async-start | bytes 15728640 | tf_op jit(solution)/shard_map/all_gather | solution.py:206
  466.0 6.0 collective-permute-start
  479.8 205.3 %collective-permute-start.1 = (bf16[2,3,512,1024]{3,2,1,0:T(8,128)(2,1)}, bf16[2,3,512,1024]{3,2,1,0:T(8,128)(2,1)}, u32[]{:S(2)}, u32[]{:S(2)}) collective-permute-start(bf16[2,3,512,1024]{3,2,1,0:T(8,128)(2,1)} %pad_maximum_fusion.1), channel_id=1, source_target_pairs={{0,2},{1,3},{2,0},{3,1},{4,6},{5,7},{6,4},{7,5},{8,10},{9,11},{10,... | collective-permute-start | bytes 18874376 | tf_op jit(solution)/shard_map/ppermute | solution.py:20
  480.3 210.2 %copy-start.45 = (s32[24]{0:T(128)}, s32[24]{0:T(128)S(1)}, u32[]{:S(2)}) copy-start(s32[24]{0:T(128)S(1)} %reshape.223) | copy-start | bytes 292
  488.5 452.0 %reduce-scatter.9.cloned.1.call-start = ((), (), s32[]{:S(2)}) async-start(), calls=%async_computation.8 | async-start | bytes 15728640 | tf_op jit(solution)/shard_map/reduce_scatter | solution.py:233
  841.3 200.8 %reduce-scatter.7.cloned.1.call-start = ((), (), s32[]{:S(2)}) async-start(), calls=%async_computation.6 | async-start | bytes 15728640 | tf_op jit(solution)/shard_map/reduce_scatter | solution.py:202
  864.1 76.4 %copy-start.26 = (f32[3,512]{1,0:T(4,128)S(1)}, f32[3,512]{1,0:T(4,128)}, u32[]{:S(2)}) copy-start(f32[3,512]{1,0:T(4,128)} %copy-done.25) | copy-start | bytes 18436
  864.1 76.4 %copy-start.28 = (f32[1024]{0:T(1024)S(1)}, f32[1024]{0:T(1024)}, u32[]{:S(2)}) copy-start(f32[1024]{0:T(1024)} %param.33) | copy-start | bytes 12292
  864.1 76.4 %copy-start.38 = (f32[1024]{0:T(1024)S(1)}, f32[1024]{0:T(1024)}, u32[]{:S(2)}) copy-start(f32[1024]{0:T(1024)} %param.40) | copy-start | bytes 12292
  864.1 82.3 %copy-start.36 = (f32[3,512]{1,0:T(4,128)S(1)}, f32[3,512]{1,0:T(4,128)}, u32[]{:S(2)}) copy-start(f32[3,512]{1,0:T(4,128)} %copy-done.35) | copy-start | bytes 18436
  864.1 82.3 %copy-start.32 = (f32[3,512]{1,0:T(4,128)S(1)}, f32[3,512]{1,0:T(4,128)}, u32[]{:S(2)}) copy-start(f32[3,512]{1,0:T(4,128)} %copy-done.31) | copy-start | bytes 18436
  864.1 275.5 %all-gather.8.cloned.1.call-start = ((), (), s32[]{:S(2)}) async-start(), calls=%async_computation.9 | async-start | bytes 15728640 | tf_op jit(solution)/shard_map/all_gather | solution.py:241
  946.4 95.7 %copy-start.50 = (f32[1024]{0:T(1024)S(1)}, f32[1024]{0:T(1024)}, u32[]{:S(2)}) copy-start(f32[1024]{0:T(1024)} %param.37) | copy-start | bytes 12292
  946.4 95.7 %copy-start.52 = (f32[3]{0:T(128)S(1)}, f32[3]{0:T(128)}, u32[]{:S(2)}) copy-start(f32[3]{0:T(128)} %copy-done.51) | copy-start | bytes 40
  1057.3 901.1 %all-reduce.5.cloned.1.call-start = ((), (), s32[]{:S(2)}) async-start(), calls=%async_computation.11 | async-start | bytes 12582912 | tf_op jit(solution)/shard_map/psum | solution.py:289
  1076.7 62.9 %copy-start.21 = (bf16[256,1024]{1,0:T(8,128)(2,1)S(1)}, bf16[256,1024]{1,0:T(8,128)(2,1)}, u32[]{:S(2)}) copy-start(bf16[256,1024]{1,0:T(8,128)(2,1)} %param.32) | copy-start | bytes 1572868
  1186.9 17.5 copy-start.6
  1743.7 315.5 %reduce-scatter.11.cloned.1.call-start = ((), (), s32[]{:S(2)}) async-start(), calls=%async_computation.10 | async-start | bytes 15728640 | tf_op jit(solution)/shard_map/reduce_scatter | solution.py:282
  1968.3 90.9 %copy-start.24 = (f32[3,512]{1,0:T(4,128)S(1)}, f32[3,512]{1,0:T(4,128)}, u32[]{:S(2)}) copy-start(f32[3,512]{1,0:T(4,128)} %copy-done.23) | copy-start | bytes 18436
  1968.3 90.9 %copy-start.40 = (f32[1024]{0:T(1024)S(1)}, f32[1024]{0:T(1024)}, u32[]{:S(2)}) copy-start(f32[1024]{0:T(1024)} %param.38) | copy-start | bytes 12292
  1974.2 89.3 %copy-start.34 = (f32[3,512]{1,0:T(4,128)S(1)}, f32[3,512]{1,0:T(4,128)}, u32[]{:S(2)}) copy-start(f32[3,512]{1,0:T(4,128)} %copy-done.33) | copy-start | bytes 18436
  1974.2 89.4 %copy-start.30 = (f32[3,512]{1,0:T(4,128)S(1)}, f32[3,512]{1,0:T(4,128)}, u32[]{:S(2)}) copy-start(f32[3,512]{1,0:T(4,128)} %copy-done.29) | copy-start | bytes 18436
  1977.9 91.2 %copy-start.41 = (f32[1024]{0:T(1024)S(1)}, f32[1024]{0:T(1024)}, u32[]{:S(2)}) copy-start(f32[1024]{0:T(1024)} %get-tuple-element.318) | copy-start | bytes 12292
  1977.9 91.2 %copy-start.42 = (f32[1024]{0:T(1024)S(1)}, f32[1024]{0:T(1024)}, u32[]{:S(2)}) copy-start(f32[1024]{0:T(1024)} %get-tuple-element.314) | copy-start | bytes 12292
  1977.9 91.2 %copy-start.43 = (f32[1024]{0:T(1024)S(1)}, f32[1024]{0:T(1024)}, u32[]{:S(2)}) copy-start(f32[1024]{0:T(1024)} %get-tuple-element.396) | copy-start | bytes 12292
  1977.9 91.2 %copy-start.44 = (f32[1024]{0:T(1024)S(1)}, f32[1024]{0:T(1024)}, u32[]{:S(2)}) copy-start(f32[1024]{0:T(1024)} %get-tuple-element.415) | copy-start | bytes 12292
  (106 other events, 664.1 us)
Sparse Core Ops, SparseCore 0:
  16.5 84.7 all-gather.3
  356.9 99.0 reduce-scatter.4
  488.6 150.7 all-gather.5
  841.4 99.0 reduce-scatter.8
  942.9 99.0 reduce-scatter.6
  1057.4 82.1 all-gather.7
  1743.8 214.5 all-reduce.4
  1961.1 97.9 reduce-scatter.10
